TPU v7x, 32 devices: a whole 2x2x4 slice. The times are simulated.
32 devices in a mesh: fsdp: 2 (over x), context: 4 (over y, core), tensor: 4 (over z).
Axes of the slice: x: 2, y: 2, z: 4, core: 2. Of those that a mesh axis runs over, the one named last changes fastest.
Arguments:
- tokens: bfloat16 [2, 2048, 1024], P('fsdp', 'context'), may hold values from -6 to 6
- cotangent: bfloat16 [2, 2048, 1024], P('fsdp', 'context'), may hold values from -6 to 6
- lengths: int32 [2, 4], P('fsdp'), may hold values from 1 to 1024, 2048 in all within a row
- w_in: bfloat16 [3, 1024, 1024], P(None, 'fsdp', 'tensor'), may hold values from -0.1875 to 0.1875
- w_out: bfloat16 [1024, 1024], P('tensor', 'fsdp'), may hold values from -0.1875 to 0.1875
- w_gate_up: bfloat16 [2, 1024, 4608], P(None, 'fsdp', 'tensor'), may hold values from -0.1875 to 0.1875
- w_down: bfloat16 [4608, 1024], P('tensor', 'fsdp'), may hold values from -0.1875 to 0.1875
- norm_gains: bfloat16 [2, 1024], P(None, 'fsdp'), may hold values from 0.5 to 1.5
- conv_kernel: bfloat16 [3, 1024], P(None, 'tensor'), may hold values from -3 to 3
Outputs:
- block_out: float32 [2, 2048, 1024], P('fsdp', 'context')
- grad_tokens: float32 [2, 2048, 1024], P('fsdp', 'context')
- grad_w_in: float32 [3, 1024, 1024], P(None, 'fsdp', 'tensor')
- grad_w_out: float32 [1024, 1024], P('tensor', 'fsdp')
- grad_w_gate_up: float32 [2, 1024, 4608], P(None, 'fsdp', 'tensor')
- grad_w_down: float32 [4608, 1024], P('tensor', 'fsdp')
- grad_norm_gains: float32 [2, 1024], P(None, 'fsdp')
- grad_conv_kernel: float32 [3, 1024], P(None, 'tensor')
Inputs may be any that keep to these rules, and one draw needn't show every extreme that they name: `lengths`: each row of 2048 tokens is a pack of 4 whole documents, in order; some document of every row has 1024 tokens.
All inputs are finite; a program needn't handle non-finite values.
Results may differ from a plain program's by a relative error of at most 0.0088.
Values may be sent and summed in bfloat16 or wider, within the bound.
No kernel may reach another device: no remote copies, remote signals or barrier semaphores. Data moves between devices by JAX's collectives and lax.ppermute only.
A program may use at most 128 MiB of HBM per device.

v0:
```python
import jax
import jax.numpy as jnp
from jax import lax
from jax.sharding import PartitionSpec as P

norm_eps = 1e-05


def shifted(block, axis, distance):
    devices = range(lax.axis_size(axis))
    route = [(i - distance, i) for i in devices if i - distance in devices]
    return lax.ppermute(block, axis, route)


def matmul_plain(matrix_one, matrix_two):
    return jnp.dot(matrix_one, matrix_two, preferred_element_type=jnp.float32)


def matmul_right(matrix_one, matrix_two):
    return lax.dot_general(
        matrix_one, matrix_two, (((1,), (1,)), ((), ())), preferred_element_type=jnp.float32
    )


def matmul_left(matrix_one, matrix_two):
    return lax.dot_general(
        matrix_one, matrix_two, (((0,), (0,)), ((), ())), preferred_element_type=jnp.float32
    )


def norm_forward(values):
    inv_root = lax.rsqrt(jnp.mean(values * values, axis=-1, keepdims=True) + norm_eps)
    return (values * inv_root, inv_root)


def norm_backward(normed, inv_root, gain_row, grad_out):
    grad_normed = grad_out * gain_row
    inner_mean = jnp.mean(grad_normed * normed, axis=-1, keepdims=True)
    return (inv_root * (grad_normed - normed * inner_mean), jnp.sum(grad_out * normed, axis=0))


def keep_masks(position, lengths_row):
    starts = jnp.cumsum(lengths_row) - lengths_row
    doc_start = jnp.max(jnp.where(starts[None, :] <= position[:, None], starts[None, :], 0), axis=1)
    keep_one = (position - 1 >= doc_start).astype(jnp.float32)[:, None]
    keep_two = (position - 2 >= doc_start).astype(jnp.float32)[:, None]
    return (keep_one, keep_two)


def local(tokens, cotangent, lengths, w_in, w_out, w_gate_up, w_down, norm_gains, conv_kernel):
    block_rows = tokens.shape[1]
    position = lax.axis_index("context") * block_rows + jnp.arange(block_rows + 2, dtype=jnp.int32)
    keep_one_ext, keep_two_ext = keep_masks(position, lengths[0])
    keep_one = keep_one_ext[:block_rows]
    keep_two = keep_two_ext[:block_rows]
    full_in, full_out, full_gate_up, full_down, full_gains = (
        lax.all_gather(w_in, "fsdp", axis=1, tiled=True),
        lax.all_gather(w_out, "fsdp", axis=1, tiled=True),
        lax.all_gather(w_gate_up, "fsdp", axis=1, tiled=True),
        lax.all_gather(w_down, "fsdp", axis=1, tiled=True),
        lax.all_gather(norm_gains, "fsdp", axis=1, tiled=True),
    )
    inputs = tokens[0].astype(jnp.float32)
    gain_first = full_gains[0].astype(jnp.float32)
    gain_second = full_gains[1].astype(jnp.float32)
    kernel_taps = conv_kernel.astype(jnp.float32)
    normed_one, root_one = norm_forward(inputs)
    hidden_one = (normed_one * gain_first).astype(jnp.bfloat16)
    b_part = matmul_plain(hidden_one, full_in[0])
    c_part = matmul_plain(hidden_one, full_in[1])
    x_part = matmul_plain(hidden_one, full_in[2])
    mixed = b_part * x_part
    rim_rows = shifted(mixed[-2:], "context", 1)
    extended = jnp.concatenate([rim_rows, mixed], axis=0)
    back_one = extended[1:-1] * keep_one
    back_two = extended[:-2] * keep_two
    conv_value = kernel_taps[2] * mixed + kernel_taps[1] * back_one + kernel_taps[0] * back_two
    gated = (c_part * conv_value).astype(jnp.bfloat16)
    first_sum = inputs + lax.psum(matmul_plain(gated, full_out), "tensor")
    normed_two, root_two = norm_forward(first_sum)
    hidden_two = (normed_two * gain_second).astype(jnp.bfloat16)
    gate_value = matmul_plain(hidden_two, full_gate_up[0])
    up_value = matmul_plain(hidden_two, full_gate_up[1])
    sigmoid_gate = jax.nn.sigmoid(gate_value)
    silu_gate = gate_value * sigmoid_gate
    act_value = (silu_gate * up_value).astype(jnp.bfloat16)
    output_rows = first_sum + lax.psum(matmul_plain(act_value, full_down), "tensor")
    full_in, full_out, full_gate_up, full_down, full_gains = (
        lax.all_gather(w_in, "fsdp", axis=1, tiled=True),
        lax.all_gather(w_out, "fsdp", axis=1, tiled=True),
        lax.all_gather(w_gate_up, "fsdp", axis=1, tiled=True),
        lax.all_gather(w_down, "fsdp", axis=1, tiled=True),
        lax.all_gather(norm_gains, "fsdp", axis=1, tiled=True),
    )
    cot_rows = cotangent[0]
    grad_act = matmul_right(cot_rows, full_down)
    grad_gate = (
        grad_act * up_value * sigmoid_gate * (1.0 + gate_value * (1.0 - sigmoid_gate))
    ).astype(jnp.bfloat16)
    grad_up = (grad_act * silu_gate).astype(jnp.bfloat16)
    grad_h2 = lax.psum(
        matmul_right(grad_gate, full_gate_up[0]) + matmul_right(grad_up, full_gate_up[1]), "tensor"
    )
    back_second, grad_gain_two = norm_backward(normed_two, root_two, gain_second, grad_h2)
    grad_first = cot_rows.astype(jnp.float32) + back_second
    grad_first_b = grad_first.astype(jnp.bfloat16)
    grad_gated = matmul_right(grad_first_b, full_out)
    grad_conv = grad_gated * c_part
    next_rows = shifted(grad_conv[:2], "context", -1)
    ahead = jnp.concatenate([grad_conv, next_rows], axis=0)
    ahead_one = ahead[1 : block_rows + 1] * keep_one_ext[1 : block_rows + 1]
    ahead_two = ahead[2:] * keep_two_ext[2:]
    grad_mixed = (
        kernel_taps[2] * grad_conv + kernel_taps[1] * ahead_one + kernel_taps[0] * ahead_two
    )
    grad_kernel = jnp.stack(
        [
            jnp.sum(grad_conv * back_two, axis=0),
            jnp.sum(grad_conv * back_one, axis=0),
            jnp.sum(grad_conv * mixed, axis=0),
        ]
    )
    grad_b = (grad_mixed * x_part).astype(jnp.bfloat16)
    grad_c = (grad_gated * conv_value).astype(jnp.bfloat16)
    grad_x = (grad_mixed * b_part).astype(jnp.bfloat16)
    local_h1 = (
        matmul_right(grad_b, full_in[0])
        + matmul_right(grad_c, full_in[1])
        + matmul_right(grad_x, full_in[2])
    )
    grad_h1 = lax.psum(local_h1, "tensor")
    back_first, grad_gain_one = norm_backward(normed_one, root_one, gain_first, grad_h1)
    grad_inputs = grad_first + back_first
    term_in = jnp.stack(
        [
            matmul_left(hidden_one, grad_b),
            matmul_left(hidden_one, grad_c),
            matmul_left(hidden_one, grad_x),
        ]
    )
    term_out = matmul_left(gated, grad_first_b)
    term_gate_up = jnp.stack([matmul_left(hidden_two, grad_gate), matmul_left(hidden_two, grad_up)])
    term_down = matmul_left(act_value, cot_rows)
    term_gains = jnp.stack([grad_gain_one, grad_gain_two])
    pieces = (
        lax.psum_scatter(term_in, "fsdp", scatter_dimension=1, tiled=True),
        lax.psum_scatter(term_out, "fsdp", scatter_dimension=1, tiled=True),
        lax.psum_scatter(term_gate_up, "fsdp", scatter_dimension=1, tiled=True),
        lax.psum_scatter(term_down, "fsdp", scatter_dimension=1, tiled=True),
        lax.psum_scatter(term_gains, "fsdp", scatter_dimension=1, tiled=True),
    )
    reduced = lax.psum((pieces[0], pieces[1], pieces[2], pieces[3], pieces[4]), "context")
    kernel_total = lax.psum(grad_kernel, ("fsdp", "context"))
    return (
        output_rows[None],
        grad_inputs[None],
        reduced[0],
        reduced[1],
        reduced[2],
        reduced[3],
        reduced[4],
        kernel_total,
    )


def solution(mesh):
    placed = (
        P("fsdp", "context", None),
        P("fsdp", "context", None),
        P("fsdp", None),
        P(None, "fsdp", "tensor"),
        P("tensor", "fsdp"),
        P(None, "fsdp", "tensor"),
        P("tensor", "fsdp"),
        P(None, "fsdp"),
        P(None, "tensor"),
    )
    return jax.shard_map(
        local,
        mesh=mesh,
        in_specs=placed,
        out_specs=(
            P("fsdp", "context", None),
            P("fsdp", "context", None),
            P(None, "fsdp", "tensor"),
            P("tensor", "fsdp"),
            P(None, "fsdp", "tensor"),
            P("tensor", "fsdp"),
            P(None, "fsdp"),
            P(None, "tensor"),
        ),
        check_vma=False,
    )
```

profile of v0, /device:TPU:0, one launch (start us, length us, event | category | flops | bytes accessed | tf_op | source)
XLA Modules:
  0.0 958.6 jit_solution(321070914398784171)
XLA Ops:
  9.4 5.5 all_gather.19
  17.5 21.9 %all-gather.4.cloned.1.call-done = bf16[3,1024,256]{2,1,0:T(8,128)(2,1)} async-done(((bf16[3,512,256]{2,1,0:T(8,128)(2,1)}), bf16[3,1024,256]{2,1,0:T(8,128)(2,1)}) %all-gather.4.cloned.1.call-update) | async-done | bytes 1572880 | tf_op jit(solution)/shard_map/all_gather | solution.py:57
  39.5 2.0 fusion.46
  44.4 8.9 all_gather.21
  58.7 84.5 %all-reduce.7.cloned.1.call-done = f32[512,1024]{1,0:T(8,128)} async-done(((f32[512,1024]{1,0:T(8,128)}), f32[512,1024]{1,0:T(8,128)}) %all-reduce.7.cloned.1.call-update) | async-done | bytes 2097168 | tf_op jit(solution)/shard_map/psum | solution.py:79
  143.2 1.9 multiply_reduce_fusion.2
  146.4 60.0 %all-gather.6.cloned.1.call-done = bf16[2,1024,1152]{2,1,0:T(8,128)(2,1)} async-done(((bf16[2,512,1152]{2,1,0:T(8,128)(2,1)}), bf16[2,1024,1152]{2,1,0:T(8,128)(2,1)}) %all-gather.6.cloned.1.call-update) | async-done | bytes 4718608 | tf_op jit(solution)/shard_map/all_gather | solution.py:59
  206.4 5.1 fusion.19
  211.5 2.9 fusion.21
  214.4 29.5 %all-gather.8.cloned.1.call-done = bf16[1152,1024]{1,0:T(8,128)(2,1)} async-done(((bf16[1152,512]{1,0:T(8,128)(2,1)}), bf16[1152,1024]{1,0:T(8,128)(2,1)}) %all-gather.8.cloned.1.call-update) | async-done | bytes 2359312 | tf_op jit(solution)/shard_map/all_gather | solution.py:60
  243.9 6.7 multiply_convert_fusion
  250.6 4.1 fusion.18
  254.6 4.5 fusion.22
  259.4 4.9 fusion.62
  264.3 81.2 %all-reduce.9.cloned.1.call-done = f32[512,1024]{1,0:T(8,128)} async-done(((f32[512,1024]{1,0:T(8,128)}), f32[512,1024]{1,0:T(8,128)}) %all-reduce.9.cloned.1.call-update) | async-done | bytes 2097168 | tf_op jit(solution)/shard_map/psum | solution.py:101
  345.5 2.3 multiply_reduce_fusion
  358.2 3.2 fusion.38
  366.6 5.2 fusion.24
  371.8 3.3 convolution_bitcast_fusion
  376.7 4.3 pad_maximum_fusion
  381.3 131.5 %all-reduce.11.cloned.1.call-done = (f32[512,1024]{1,0:T(8,128)}, f32[512,1024]{1,0:T(8,128)}) async-done(((f32[512,1024]{1,0:T(8,128)}, f32[512,1024]{1,0:T(8,128)}), (f32[512,1024]{1,0:T(8,128)}, f32[512,1024]{1,0:T(8,128)})) %all-reduce.11.cloned.1.call-update) | async-done | bytes 4194320 | tf_op jit(solution)/shard_map/psum | solution.py:87
  512.8 2.2 fusion.14
  516.2 18.3 %reduce-scatter.10.cloned.1.call-done = f32[256,512]{1,0:T(8,128)} async-done(((f32[256,1024]{1,0:T(8,128)}), f32[256,512]{1,0:T(8,128)}) %reduce-scatter.10.cloned.1.call-update) | async-done | bytes 524304 | tf_op jit(solution)/shard_map/reduce_scatter | solution.py:147
  534.4 45.7 %reduce-scatter.8.cloned.1.call-done = f32[3,512,256]{2,1,0:T(8,128)} async-done(((f32[3,1024,256]{2,1,0:T(8,128)}), f32[3,512,256]{2,1,0:T(8,128)}) %reduce-scatter.8.cloned.1.call-update) | async-done | bytes 1572880 | tf_op jit(solution)/shard_map/reduce_scatter | solution.py:146
  580.1 63.0 %reduce-scatter.14.cloned.1.call-done = f32[1152,512]{1,0:T(8,128)} async-done(((f32[1152,1024]{1,0:T(8,128)}), f32[1152,512]{1,0:T(8,128)}) %reduce-scatter.14.cloned.1.call-update) | async-done | bytes 2359312 | tf_op jit(solution)/shard_map/reduce_scatter | solution.py:149
  643.1 112.8 %reduce-scatter.12.cloned.1.call-done = f32[2,512,1152]{2,1,0:T(8,128)} async-done(((f32[2,1024,1152]{2,1,0:T(8,128)}), f32[2,512,1152]{2,1,0:T(8,128)}) %reduce-scatter.12.cloned.1.call-update) | async-done | bytes 4718608 | tf_op jit(solution)/shard_map/reduce_scatter | solution.py:148
  756.0 13.1 %psum.79 = f32[3,256]{1,0:T(4,128)} all-reduce(f32[3,256]{1,0:T(4,128)S(1)} %pad_maximum_fusion.5), channel_id=1, replica_groups=mesh['fsdp'=2,'context'=4,'tensor'=4] {'fsdp','context'}, use_global_device_ids=true, to_apply=%region_25.26 | all-reduce | flops 768 | bytes 6144 | tf_op jit(solution)/shard_map/psum | solution.py:153
  769.1 3.6 add_bitcast_fusion
  775.8 6.3 psum.78
  782.1 159.7 %all-reduce.13.cloned.1.call-done = (f32[3,512,256]{2,1,0:T(8,128)}, f32[256,512]{1,0:T(8,128)}, f32[2,512,1152]{2,1,0:T(8,128)}, f32[1152,512]{1,0:T(8,128)}) async-done(((f32[3,512,256]{2,1,0:T(8,128)}, f32[256,512]{1,0:T(8,128)}, f32[2,512,1152]{2,1,0:T(8,128)}, f32[1152,512]{1,0:T(8,128)}), (f32[3,512,256]{2,1,0:T(8,128)}, f32[256,512]{1,0:T(8,128)}, f32[2,512,1152]{2,1,0:T(8,128)}, ...) | async-done | bytes 9175056 | tf_op jit(solution)/shard_map/psum | solution.py:152
  941.8 2.7 copy.27
  945.3 5.0 copy.29
  (128 shorter events, 38.2 us)
Async XLA Ops:
  7.2 32.3 %all-gather.4.cloned.1.call-start = ((), (), s32[]{:S(2)}) async-start(), calls=%async_computation.5 | async-start | bytes 2359296 | tf_op jit(solution)/shard_map/all_gather | solution.py:57
  7.9 135.3 %all-reduce.7.cloned.1.call-start = ((), (), s32[]{:S(2)}) async-start(), calls=%async_computation.6 | async-start | bytes 4194304 | tf_op jit(solution)/shard_map/psum | solution.py:79
  15.0 26.4 %copy-start.2 = (bf16[1,512,1024]{2,1,0:T(8,128)(2,1)S(1)}, bf16[1,512,1024]{2,1,0:T(8,128)(2,1)}, u32[]{:S(2)}) copy-start(bf16[1,512,1024]{2,1,0:T(8,128)(2,1)} %param.9) | copy-start | bytes 3145732
  41.5 2.9 copy-start.28
  42.8 12.1 %copy-start.20 = (f32[512,256]{1,0:T(8,128)}, f32[512,256]{1,0:T(8,128)S(1)}, u32[]{:S(2)}) copy-start(f32[512,256]{1,0:T(8,128)S(1)} %get-tuple-element.43) | copy-start | bytes 1572868
  42.8 10.5 %collective-permute-start = (f32[2,256]{1,0:T(2,128)S(1)}, f32[2,256]{1,0:T(2,128)S(1)}, u32[]{:S(2)}, u32[]{:S(2)}) collective-permute-start(f32[2,256]{1,0:T(2,128)S(1)} %slice.98), channel_id=1, source_target_pairs={{0,4},{4,8},{8,12},{1,5},{5,9},{9,13},{2,6},{6,10},{10,14},{3,7},{... | collective-permute-start | bytes 6152 | tf_op jit(solution)/shard_map/ppermute | solution.py:12
  57.3 149.1 %all-gather.6.cloned.1.call-start = ((), (), s32[]{:S(2)}) async-start(), calls=%async_computation.7 | async-start | bytes 7077888 | tf_op jit(solution)/shard_map/all_gather | solution.py:59
  58.1 185.8 %all-gather.8.cloned.1.call-start = ((), (), s32[]{:S(2)}) async-start(), calls=%async_computation.8 | async-start | bytes 3538944 | tf_op jit(solution)/shard_map/all_gather | solution.py:60
  58.7 286.9 %all-reduce.9.cloned.1.call-start = ((), (), s32[]{:S(2)}) async-start(), calls=%async_computation.9 | async-start | bytes 4194304 | tf_op jit(solution)/shard_map/psum | solution.py:101
  206.4 5.1 copy-start.3
  206.4 5.1 copy-start.29
  250.5 4.1 copy-start.13
  250.5 4.1 copy-start.15
  259.2 253.6 %all-reduce.11.cloned.1.call-start = ((), (), s32[]{:S(2)}) async-start(), calls=%async_computation.15 | async-start | bytes 8388608 | tf_op jit(solution)/shard_map/psum | solution.py:87
  345.5 2.5 copy-start.9
  349.1 2.4 copy-start
  349.6 3.4 copy-start.12
  351.5 3.5 copy-start.19
  351.5 3.2 copy-start.22
  351.5 3.2 collective-permute-start.1
  358.1 176.3 %reduce-scatter.10.cloned.1.call-start = ((), (), s32[]{:S(2)}) async-start(), calls=%async_computation.11 | async-start | bytes 1572864 | tf_op jit(solution)/shard_map/reduce_scatter | solution.py:147
  361.4 218.7 %reduce-scatter.8.cloned.1.call-start = ((), (), s32[]{:S(2)}) async-start(), calls=%async_computation.10 | async-start | bytes 4718592 | tf_op jit(solution)/shard_map/reduce_scatter | solution.py:146
  366.5 276.6 %reduce-scatter.14.cloned.1.call-start = ((), (), s32[]{:S(2)}) async-start(), calls=%async_computation.13 | async-start | bytes 7077888 | tf_op jit(solution)/shard_map/reduce_scatter | solution.py:149
  371.8 384.2 %reduce-scatter.12.cloned.1.call-start = ((), (), s32[]{:S(2)}) async-start(), calls=%async_computation.12 | async-start | bytes 14155776 | tf_op jit(solution)/shard_map/reduce_scatter | solution.py:148
  371.8 3.3 copy-start.4
  371.8 3.3 copy-start.14
  381.0 393.7 %reduce-scatter.16.cloned.1.call-start = ((), (), s32[]{:S(2)}) async-start(), calls=%async_computation.14 | async-start | bytes 786432
  516.1 425.7 %all-reduce.13.cloned.1.call-start = ((), (), s32[]{:S(2)}) async-start(), calls=%async_computation.16 | async-start | bytes 18350080 | tf_op jit(solution)/shard_map/psum | solution.py:152
  769.1 3.6 copy-start.1
  769.1 3.6 copy-start.6
  941.8 2.7 copy-start.25
  945.3 5.0 copy-start.10
  (12 other events, 18.2 us)
Sparse Core Ops, SparseCore 0:
  9.5 29.8 all-gather.3
  57.5 85.6 all-reduce.6
  144.7 61.6 all-gather.5
  207.8 36.0 all-gather.7
  259.3 86.1 all-reduce.8
  358.2 154.5 all-reduce.10
  515.0 19.3 reduce-scatter.9
  536.7 43.3 reduce-scatter.7
  583.0 60.0 reduce-scatter.13
  645.3 110.6 reduce-scatter.11
  758.8 14.6 reduce-scatter.15
  776.1 165.6 all-reduce.12
where the time goes:
time: 959 us
  waiting for transfers between devices  811 us (85%)
  matrix products  54 us (6%)
  blocking collectives  33.8 us (4%)
  other arithmetic  23.9 us (2%)
  local copies, waits for them, and re-layouts  17 us (2%)
  between operations  14.6 us (2%)
    psum x1, waiting for transfers between devices, local(): lax.psum((pieces[0], pieces[1], pieces[2], pieces[3], pieces[4]), 'context')  160 us
    psum x1, waiting for transfers between devices, local(): lax.psum(matmul_plain(act_value, full_down), 'tensor')  131 us
    reduce_scatter x1, waiting for transfers between devices, local(): lax.psum_scatter(term_gate_up, 'fsdp', scatter_dimension=1, tiled=True)  113 us
    psum x1, waiting for transfers between devices, local(): first_sum = inputs + lax.psum(matmul_plain(gated, full_out), 'tensor')  84.5 us
    psum x1, waiting for transfers between devices, local(): lax.psum(matmul_right(grad_gate, full_gate_up[0]) + matmul_right(grad_up,...  81.2 us
    reduce_scatter x1, waiting for transfers between devices, local(): lax.psum_scatter(term_down, 'fsdp', scatter_dimension=1, tiled=True)  63 us
    all_gather x1, waiting for transfers between devices, local(): lax.all_gather(w_gate_up, 'fsdp', axis=1, tiled=True)  60 us
    reduce_scatter x1, waiting for transfers between devices, local(): lax.psum_scatter(term_in, 'fsdp', scatter_dimension=1, tiled=True)  45.7 us
  transfers between devices with their start and end apart: 14, of which 12 were waited for; matrix products, arithmetic and copies ran while one was open for 5% of the time, Pallas kernels for 0%

commit v1 on v0

--- a/solution.py
+++ b/solution.py
@@ -4,6 +4,12 @@
 from jax.sharding import PartitionSpec as P
 
 norm_eps = 1e-05
+
+
+def gather_and_add(value, axis):
+    terms = lax.all_gather(value, axis, axis=0, tiled=False)
+    acc = terms.sum(axis=0)
+    return acc
 
 
 def shifted(block, axis, distance):
@@ -76,7 +82,7 @@
     back_two = extended[:-2] * keep_two
     conv_value = kernel_taps[2] * mixed + kernel_taps[1] * back_one + kernel_taps[0] * back_two
     gated = (c_part * conv_value).astype(jnp.bfloat16)
-    first_sum = inputs + lax.psum(matmul_plain(gated, full_out), "tensor")
+    first_sum = inputs + gather_and_add(matmul_plain(gated, full_out), "tensor")
     normed_two, root_two = norm_forward(first_sum)
     hidden_two = (normed_two * gain_second).astype(jnp.bfloat16)
     gate_value = matmul_plain(hidden_two, full_gate_up[0])

time: 959 us -> 1020 us (1.064)
  waiting for transfers between devices: 811 us -> 868 us
    all_gather x0 -> x1, waiting for transfers between devices: none -> 148 us  [gather_and_add(): terms = lax.all_gather(value, axis, axis=0, tiled=False)]
    psum x1 -> x0, waiting for transfers between devices: 84.5 us -> none  [local(): first_sum = inputs + lax.psum(matmul_plain(gated, full_out), 'tensor')]
  transfers between devices with their start and end apart: 14 -> 14, of which waited for: 12 -> 12; matrix products, arithmetic and copies ran while one was open for 5% -> 6% of each run, Pallas kernels for 0% -> 0%
where the time goes in v1:
time: 1020 us
  waiting for transfers between devices  868 us (85%)
  matrix products  53.8 us (5%)
  blocking collectives  33.9 us (3%)
  other arithmetic  30.1 us (3%)
  local copies, waits for them, and re-layouts  17.4 us (2%)
  between operations  14.5 us (1%)
    psum x1, waiting for transfers between devices, local(): lax.psum((pieces[0], pieces[1], pieces[2], pieces[3], pieces[4]), 'context')  160 us
    all_gather x1, waiting for transfers between devices, gather_and_add(): terms = lax.all_gather(value, axis, axis=0, tiled=False)  148 us
    psum x1, waiting for transfers between devices, local(): lax.psum(matmul_plain(act_value, full_down), 'tensor')  132 us
    reduce_scatter x1, waiting for transfers between devices, local(): lax.psum_scatter(term_gate_up, 'fsdp', scatter_dimension=1, tiled=True)  113 us
    psum x1, waiting for transfers between devices, local(): lax.psum(matmul_right(grad_gate, full_gate_up[0]) + matmul_right(grad_up,...  81.2 us
    reduce_scatter x1, waiting for transfers between devices, local(): lax.psum_scatter(term_down, 'fsdp', scatter_dimension=1, tiled=True)  63 us
    all_gather x1, waiting for transfers between devices, local(): lax.all_gather(w_gate_up, 'fsdp', axis=1, tiled=True)  52.3 us
    reduce_scatter x1, waiting for transfers between devices, local(): lax.psum_scatter(term_in, 'fsdp', scatter_dimension=1, tiled=True)  45.7 us
  transfers between devices with their start and end apart: 14, of which 12 were waited for; matrix products, arithmetic and copies ran while one was open for 6% of the time, Pallas kernels for 0%

profile of v1, /device:TPU:0, one launch (start us, length us, event | category | flops | bytes accessed | tf_op | source)
XLA Modules:
  0.0 1021.1 jit_solution(15162387970060687774)
XLA Ops:
  9.4 5.5 all_gather.25
  17.5 21.9 %all-gather.6.cloned.1.call-done = bf16[3,1024,256]{2,1,0:T(8,128)(2,1)} async-done(((bf16[3,512,256]{2,1,0:T(8,128)(2,1)}), bf16[3,1024,256]{2,1,0:T(8,128)(2,1)}) %all-gather.6.cloned.1.call-update) | async-done | bytes 1572880 | tf_op jit(solution)/shard_map/all_gather | solution.py:63
  44.3 8.9 all_gather.27
  58.7 147.9 %all-gather.12.cloned.1.call-done = f32[2048,1024]{1,0:T(8,128)} async-done(((f32[512,1024]{1,0:T(8,128)}), f32[2048,1024]{1,0:T(8,128)}) %all-gather.12.cloned.1.call-update) | async-done | bytes 8388624 | tf_op jit(solution)/shard_map/all_gather | solution.py:10
  206.6 5.9 reduce_sum.93
  212.5 2.4 multiply_reduce_fusion.2
  216.7 52.3 %all-gather.8.cloned.1.call-done = bf16[2,1024,1152]{2,1,0:T(8,128)(2,1)} async-done(((bf16[2,512,1152]{2,1,0:T(8,128)(2,1)}), bf16[2,1024,1152]{2,1,0:T(8,128)(2,1)}) %all-gather.8.cloned.1.call-update) | async-done | bytes 4718608 | tf_op jit(solution)/shard_map/all_gather | solution.py:65
  269.0 5.1 fusion.22
  274.1 2.9 fusion.24
  277.0 29.5 %all-gather.10.cloned.1.call-done = bf16[1152,1024]{1,0:T(8,128)(2,1)} async-done(((bf16[1152,512]{1,0:T(8,128)(2,1)}), bf16[1152,1024]{1,0:T(8,128)(2,1)}) %all-gather.10.cloned.1.call-update) | async-done | bytes 2359312 | tf_op jit(solution)/shard_map/all_gather | solution.py:66
  306.5 6.7 multiply_convert_fusion
  313.1 4.1 fusion.21
  317.2 4.5 fusion.25
  322.0 4.9 fusion.66
  326.9 81.2 %all-reduce.6.cloned.1.call-done = f32[512,1024]{1,0:T(8,128)} async-done(((f32[512,1024]{1,0:T(8,128)}), f32[512,1024]{1,0:T(8,128)}) %all-reduce.6.cloned.1.call-update) | async-done | bytes 2097168 | tf_op jit(solution)/shard_map/psum | solution.py:107
  408.1 2.3 multiply_reduce_fusion
  420.7 3.2 fusion.42
  429.1 5.2 fusion.28
  434.4 3.0 convolution_bitcast_fusion
  439.1 4.3 pad_maximum_fusion
  443.7 131.7 %all-reduce.8.cloned.1.call-done = (f32[512,1024]{1,0:T(8,128)}, f32[512,1024]{1,0:T(8,128)}) async-done(((f32[512,1024]{1,0:T(8,128)}, f32[512,1024]{1,0:T(8,128)}), (f32[512,1024]{1,0:T(8,128)}, f32[512,1024]{1,0:T(8,128)})) %all-reduce.8.cloned.1.call-update) | async-done | bytes 4194320 | tf_op jit(solution)/shard_map/psum | solution.py:93
  575.4 2.3 fusion.14
  578.7 18.3 %reduce-scatter.10.cloned.1.call-done = f32[256,512]{1,0:T(8,128)} async-done(((f32[256,1024]{1,0:T(8,128)}), f32[256,512]{1,0:T(8,128)}) %reduce-scatter.10.cloned.1.call-update) | async-done | bytes 524304 | tf_op jit(solution)/shard_map/reduce_scatter | solution.py:153
  597.0 45.7 %reduce-scatter.8.cloned.1.call-done = f32[3,512,256]{2,1,0:T(8,128)} async-done(((f32[3,1024,256]{2,1,0:T(8,128)}), f32[3,512,256]{2,1,0:T(8,128)}) %reduce-scatter.8.cloned.1.call-update) | async-done | bytes 1572880 | tf_op jit(solution)/shard_map/reduce_scatter | solution.py:152
  642.7 63.0 %reduce-scatter.14.cloned.1.call-done = f32[1152,512]{1,0:T(8,128)} async-done(((f32[1152,1024]{1,0:T(8,128)}), f32[1152,512]{1,0:T(8,128)}) %reduce-scatter.14.cloned.1.call-update) | async-done | bytes 2359312 | tf_op jit(solution)/shard_map/reduce_scatter | solution.py:155
  705.7 112.8 %reduce-scatter.12.cloned.1.call-done = f32[2,512,1152]{2,1,0:T(8,128)} async-done(((f32[2,1024,1152]{2,1,0:T(8,128)}), f32[2,512,1152]{2,1,0:T(8,128)}) %reduce-scatter.12.cloned.1.call-update) | async-done | bytes 4718608 | tf_op jit(solution)/shard_map/reduce_scatter | solution.py:154
  818.5 13.1 %psum.71 = f32[3,256]{1,0:T(4,128)} all-reduce(f32[3,256]{1,0:T(4,128)S(1)} %pad_maximum_fusion.5), channel_id=1, replica_groups=mesh['fsdp'=2,'context'=4,'tensor'=4] {'fsdp','context'}, use_global_device_ids=true, to_apply=%region_25.26 | all-reduce | flops 768 | bytes 6144 | tf_op jit(solution)/shard_map/psum | solution.py:159
  831.7 3.5 add_bitcast_fusion
  838.1 6.4 psum.70
  844.5 159.9 %all-reduce.10.cloned.1.call-done = (f32[3,512,256]{2,1,0:T(8,128)}, f32[256,512]{1,0:T(8,128)}, f32[2,512,1152]{2,1,0:T(8,128)}, f32[1152,512]{1,0:T(8,128)}) async-done(((f32[3,512,256]{2,1,0:T(8,128)}, f32[256,512]{1,0:T(8,128)}, f32[2,512,1152]{2,1,0:T(8,128)}, f32[1152,512]{1,0:T(8,128)}), (f32[3,512,256]{2,1,0:T(8,128)}, f32[256,512]{1,0:T(8,128)}, f32[2,512,1152]{2,1,0:T(8,128)}, ...) | async-done | bytes 9175056 | tf_op jit(solution)/shard_map/psum | solution.py:158
  1004.4 2.7 copy.26
  1007.9 5.0 copy.28
  (129 shorter events, 40.7 us)
Async XLA Ops:
  7.2 32.3 %all-gather.6.cloned.1.call-start = ((), (), s32[]{:S(2)}) async-start(), calls=%async_computation.5 | async-start | bytes 2359296 | tf_op jit(solution)/shard_map/all_gather | solution.py:63
  7.9 198.7 %all-gather.12.cloned.1.call-start = ((), (), s32[]{:S(2)}) async-start(), calls=%async_computation.13 | async-start | bytes 10485760 | tf_op jit(solution)/shard_map/all_gather | solution.py:10
  15.0 26.4 %copy-start.2 = (bf16[1,512,1024]{2,1,0:T(8,128)(2,1)S(1)}, bf16[1,512,1024]{2,1,0:T(8,128)(2,1)}, u32[]{:S(2)}) copy-start(bf16[1,512,1024]{2,1,0:T(8,128)(2,1)} %param.9) | copy-start | bytes 3145732
  41.5 11.8 %copy-start.20 = (f32[512,256]{1,0:T(8,128)}, f32[512,256]{1,0:T(8,128)S(1)}, u32[]{:S(2)}) copy-start(f32[512,256]{1,0:T(8,128)S(1)} %fusion.50) | copy-start | bytes 1572868
  41.5 2.9 copy-start.25
  42.8 12.1 %copy-start.17 = (f32[512,256]{1,0:T(8,128)}, f32[512,256]{1,0:T(8,128)S(1)}, u32[]{:S(2)}) copy-start(f32[512,256]{1,0:T(8,128)S(1)} %get-tuple-element.43) | copy-start | bytes 1572868
  42.8 10.5 %collective-permute-start = (f32[2,256]{1,0:T(2,128)S(1)}, f32[2,256]{1,0:T(2,128)S(1)}, u32[]{:S(2)}, u32[]{:S(2)}) collective-permute-start(f32[2,256]{1,0:T(2,128)S(1)} %slice.98), channel_id=1, source_target_pairs={{0,4},{4,8},{8,12},{1,5},{5,9},{9,13},{2,6},{6,10},{10,14},{3,7},{... | collective-permute-start | bytes 6152 | tf_op jit(solution)/shard_map/ppermute | solution.py:18
  57.3 211.7 %all-gather.8.cloned.1.call-start = ((), (), s32[]{:S(2)}) async-start(), calls=%async_computation.6 | async-start | bytes 7077888 | tf_op jit(solution)/shard_map/all_gather | solution.py:65
  58.1 248.4 %all-gather.10.cloned.1.call-start = ((), (), s32[]{:S(2)}) async-start(), calls=%async_computation.7 | async-start | bytes 3538944 | tf_op jit(solution)/shard_map/all_gather | solution.py:66
  58.6 349.5 %all-reduce.6.cloned.1.call-start = ((), (), s32[]{:S(2)}) async-start(), calls=%async_computation.8 | async-start | bytes 4194304 | tf_op jit(solution)/shard_map/psum | solution.py:107
  212.5 2.8 copy-start.3
  269.0 5.1 copy-start.12
  269.0 5.1 copy-start.26
  313.1 4.1 copy-start.27
  313.1 4.1 copy-start.29
  321.8 253.6 %all-reduce.8.cloned.1.call-start = ((), (), s32[]{:S(2)}) async-start(), calls=%async_computation.15 | async-start | bytes 8388608 | tf_op jit(solution)/shard_map/psum | solution.py:93
  408.1 2.5 copy-start.8
  412.1 3.4 copy-start.11
  414.1 3.5 copy-start.16
  414.1 3.2 copy-start.19
  414.1 3.2 collective-permute-start.1
  420.7 176.3 %reduce-scatter.10.cloned.1.call-start = ((), (), s32[]{:S(2)}) async-start(), calls=%async_computation.10 | async-start | bytes 1572864 | tf_op jit(solution)/shard_map/reduce_scatter | solution.py:153
  424.0 218.7 %reduce-scatter.8.cloned.1.call-start = ((), (), s32[]{:S(2)}) async-start(), calls=%async_computation.9 | async-start | bytes 4718592 | tf_op jit(solution)/shard_map/reduce_scatter | solution.py:152
  429.1 276.6 %reduce-scatter.14.cloned.1.call-start = ((), (), s32[]{:S(2)}) async-start(), calls=%async_computation.12 | async-start | bytes 7077888 | tf_op jit(solution)/shard_map/reduce_scatter | solution.py:155
  434.3 384.2 %reduce-scatter.12.cloned.1.call-start = ((), (), s32[]{:S(2)}) async-start(), calls=%async_computation.11 | async-start | bytes 14155776 | tf_op jit(solution)/shard_map/reduce_scatter | solution.py:154
  434.4 3.0 copy-start.28
  443.4 393.7 %reduce-scatter.16.cloned.1.call-start = ((), (), s32[]{:S(2)}) async-start(), calls=%async_computation.14 | async-start | bytes 786432
  578.7 425.7 %all-reduce.10.cloned.1.call-start = ((), (), s32[]{:S(2)}) async-start(), calls=%async_computation.16 | async-start | bytes 18350080 | tf_op jit(solution)/shard_map/psum | solution.py:158
  831.7 3.5 copy-start.1
  831.7 3.5 copy-start.5
  1004.4 2.7 copy-start.22
  1007.9 5.0 copy-start.9
  (12 other events, 19.3 us)
Sparse Core Ops, SparseCore 0:
  9.5 29.8 all-gather.5
  57.4 149.1 all-gather.11
  208.2 60.8 all-gather.7
  270.4 36.0 all-gather.9
  321.9 86.1 all-reduce.5
  420.8 154.4 all-reduce.7
  577.6 19.3 reduce-scatter.9
  599.2 43.3 reduce-scatter.7
  645.6 60.0 reduce-scatter.13
  707.8 110.6 reduce-scatter.11
  821.3 14.6 reduce-scatter.15
  838.7 165.6 all-reduce.9
